TPU v7x, 256 devices: a whole 4x4x8 slice. The times are simulated.
256 devices in a mesh: tok: 16 (over y_lo, x, core), mdl: 16 (over y_hi, z).
Axes of the slice: x: 4, y: 4 (y_hi: 2, y_lo: 2; y = y_hi * 2 + y_lo), z: 8, core: 2. Of those that a mesh axis runs over, the one named last changes fastest.
Arguments:
- hidden: bfloat16 [8192, 2048], P('tok'), may hold values from -40 to 40
- segment_ids: int32 [8192], replicated, may hold values from 0 to 3, never falling along the last dimension, each value on 1 to 4096 neighbouring positions
- routes: int32 [8192, 2], P('tok'), may hold values from 0 to 7, all different within a row; in each aligned block of 512 rows (0 to 511, 512 to 1023, ...) at most 256 rows name the same one
- norm_gain: float32 [2048], replicated, may hold values from 0.5 to 1.5
- router_weight: float32 [2048, 8], replicated, may hold values from -0.125 to 0.125
- query_weight: bfloat16 [8, 2048, 2048], P(None, 'tok', 'mdl'), may hold values from -2 to 2
- kv_weight: bfloat16 [2, 2048, 2048], P(None, 'tok', 'mdl'), may hold values from -16 to 16
- out_weight: bfloat16 [8, 2048, 2048], P(None, 'mdl', 'tok'), may hold values from -0.5 to 0.5
- page_table: int32 [512], P('tok'), may hold values from 0 to 511, as said below
Outputs:
- output: bfloat16 [8192, 2048], P('tok', 'mdl')
- cache: bfloat16 [512, 16, 2, 2048], P('tok', None, None, 'mdl')
Inputs may be any that keep to these rules, and one draw needn't show every extreme that they name: `segment_ids`: Non-decreasing along the tokens; every prompt number 0 to 3 occurs, each prompt 1 to 4096 tokens long, one exactly 4096. `routes`: each token names 2 different experts; among the 512 tokens of an aligned block no expert is named more than 256 times, and some block reaches 256. `page_table`: A permutation of the 512 physical pages; of the 32 logical pages of each aligned block, exactly 2 lie in each aligned range of 32 physical pages.
All inputs are finite; a program needn't handle non-finite values.
Results may differ from a plain program's by a relative error of at most 0.019.
Values may be sent and summed in bfloat16 or wider, within the bound.
No kernel may reach another device: no remote copies, remote signals or barrier semaphores. Data moves between devices by JAX's collectives and lax.ppermute only.
A program may use at most 128 MiB of HBM per device.

v0:
```python
import math
import jax
import jax.numpy as jnp
from jax import lax
from jax.sharding import PartitionSpec as P

HDIM = 128
SEGS = 4
EPSILON = 1e-05
MASKED = -1e30


def rms_norm(hidden, norm_gain):
    values = hidden.astype(jnp.float32)
    factor = lax.rsqrt(jnp.mean(values * values, axis=-1, keepdims=True) + EPSILON)
    return (values * factor * norm_gain).astype(jnp.bfloat16)


def route_gates(normed, router_weight, routes):
    logits = jnp.dot(normed.astype(jnp.float32), router_weight, precision=lax.Precision.HIGHEST)
    expert_ids = jnp.arange(logits.shape[1], dtype=jnp.int32)
    picked = routes[:, :, None] == expert_ids[None, None, :]
    chosen = jnp.sum(jnp.where(picked, logits[:, None, :], jnp.float32(0.0)), axis=-1)
    return jax.nn.softmax(chosen, axis=-1)


def place_pages(key_values, page_table, shards, tok_row):
    pages_here = page_table.shape[0]
    per_peer = pages_here // shards
    page_rows = key_values.shape[0] // pages_here
    head_cols = key_values.shape[2]
    targets = page_table // pages_here
    onehot = (targets[:, None] == jnp.arange(shards, dtype=jnp.int32)[None, :]).astype(jnp.int32)
    ranks = jnp.sum((jnp.cumsum(onehot, axis=0) - 1) * onehot, axis=1)
    ordering = (
        jnp.zeros((pages_here,), jnp.int32)
        .at[targets * per_peer + ranks]
        .set(jnp.arange(pages_here, dtype=jnp.int32))
    )
    outgoing = key_values.reshape(pages_here, page_rows, 2, head_cols)[ordering].reshape(
        shards, per_peer, page_rows, 2, head_cols
    )
    labels = page_table[ordering].reshape(shards, per_peer)
    incoming, got_labels = (
        lax.all_to_all(outgoing, "tok", split_axis=0, concat_axis=0, tiled=True),
        lax.all_to_all(labels, "tok", split_axis=0, concat_axis=0, tiled=True),
    )
    places = got_labels.reshape(-1) - tok_row * pages_here
    arrived = incoming.reshape(pages_here, page_rows, 2, head_cols)
    return jnp.zeros((pages_here, page_rows, 2, head_cols), jnp.bfloat16).at[places].set(arrived)


def local(
    hidden,
    segment_ids,
    routes,
    norm_gain,
    router_weight,
    query_weight,
    kv_weight,
    out_weight,
    page_table,
):
    tok_dev, width = hidden.shape
    experts = query_weight.shape[0]
    head_cols = query_weight.shape[2]
    heads_here = head_cols // HDIM
    capacity = tok_dev // 2
    top_count = routes.shape[1]
    assigned = tok_dev * top_count
    shards = lax.axis_size("tok")
    tok_row = lax.axis_index("tok")
    normed = rms_norm(hidden, norm_gain)
    gates = route_gates(normed, router_weight, routes)
    flat_expert = routes.reshape(-1)
    expert_ids = jnp.arange(experts, dtype=jnp.int32)
    onehot = (flat_expert[:, None] == expert_ids[None, :]).astype(jnp.int32)
    ranks = jnp.sum((jnp.cumsum(onehot, axis=0) - 1) * onehot, axis=1)
    slots = flat_expert * capacity + ranks
    assign_ids = jnp.arange(assigned, dtype=jnp.int32)
    slot_assign = jnp.zeros((experts * capacity,), jnp.int32).at[slots].set(assign_ids)
    slot_token = slot_assign // top_count
    slot_filled = jnp.zeros((experts * capacity,), jnp.bfloat16).at[slots].set(jnp.bfloat16(1.0))
    slot_gate = jnp.zeros((experts * capacity,), jnp.float32).at[slots].set(gates.reshape(-1))
    grouped = (normed[slot_token] * slot_filled[:, None]).reshape(experts, capacity, width)
    query_part = lax.all_gather(query_weight, "tok", axis=1, tiled=True)
    key_part = lax.all_gather(kv_weight, "tok", axis=1, tiled=True)
    query_total = jnp.einsum(
        "ecd,edh->ech", grouped, query_part, preferred_element_type=jnp.float32
    )
    key_total = jnp.einsum("td,kdh->tkh", normed, key_part, preferred_element_type=jnp.float32)
    queries = query_total.astype(jnp.bfloat16).reshape(experts * capacity, head_cols)[slots]
    key_values = key_total.astype(jnp.bfloat16)
    cache = place_pages(key_values, page_table, shards, tok_row)
    by_head_q = queries.reshape(assigned, heads_here, HDIM).transpose(1, 0, 2)
    q_pos = tok_row * tok_dev + assign_ids // top_count
    q_seg = segment_ids[q_pos]
    prompt_ids = jnp.arange(SEGS, dtype=jnp.int32)
    seg_first = jnp.sum((segment_ids[:, None] < prompt_ids[None, :]).astype(jnp.int32), axis=0)
    q_lower = jnp.sum(
        jnp.where(q_seg[:, None] == prompt_ids[None, :], seg_first[None, :], 0), axis=1
    )
    start_state = (
        jnp.full((heads_here, assigned), MASKED, jnp.float32),
        jnp.zeros((heads_here, assigned), jnp.float32),
        jnp.zeros((heads_here, assigned, HDIM), jnp.float32),
    )
    state = start_state
    piece = lax.all_gather(key_values, "tok", axis=0, tiled=True)
    count = piece.shape[0]
    block = math.gcd(count, 512)
    key_blocks = piece[:, 0].reshape(count // block, block, heads_here, HDIM)
    value_blocks = piece[:, 1].reshape(count // block, block, heads_here, HDIM)
    firsts = block * jnp.arange(count // block, dtype=jnp.int32)

    def one_block(carry, inputs):
        peak, total, accum = carry
        key_block, value_block, first = inputs
        k_pos = first + jnp.arange(block, dtype=jnp.int32)
        allowed = (k_pos[None, :] >= q_lower[:, None]) & (k_pos[None, :] <= q_pos[:, None])
        scores = jnp.einsum(
            "hqd,khd->hqk", by_head_q, key_block, preferred_element_type=jnp.float32
        ) / math.sqrt(HDIM)
        scores = jnp.where(allowed[None], scores, jnp.float32(MASKED))
        new_peak = jnp.maximum(peak, jnp.max(scores, axis=-1))
        shrink = jnp.exp(peak - new_peak)
        expon = jnp.where(allowed[None], jnp.exp(scores - new_peak[..., None]), jnp.float32(0.0))
        total = total * shrink + jnp.sum(expon, axis=-1)
        accum = accum * shrink[..., None] + jnp.einsum(
            "hqk,khd->hqd",
            expon.astype(jnp.bfloat16),
            value_block,
            preferred_element_type=jnp.float32,
        )
        return ((new_peak, total, accum), None)

    state, _ = lax.scan(one_block, state, (key_blocks, value_blocks, firsts))
    attended = (
        (state[2] / state[1][..., None])
        .astype(jnp.bfloat16)
        .transpose(1, 0, 2)
        .reshape(assigned, head_cols)
    )
    grouped_out = (attended[slot_assign] * slot_filled[:, None]).reshape(
        experts, capacity, head_cols
    )
    piece = lax.all_gather(out_weight, "tok", axis=2, tiled=True)
    count = piece.shape[2]
    terms = jnp.einsum(
        "ech,ehn->ecn", grouped_out, piece, preferred_element_type=jnp.float32
    ).reshape(experts * capacity, count)
    partial_sums = (
        jnp.zeros((tok_dev, count), jnp.float32).at[slot_token].add(terms * slot_gate[:, None])
    )
    mine = lax.psum_scatter(
        partial_sums.astype(jnp.bfloat16), "mdl", scatter_dimension=1, tiled=True
    ).astype(jnp.float32)
    span = width // lax.axis_size("mdl")
    residual_part = lax.dynamic_slice_in_dim(hidden, lax.axis_index("mdl") * span, span, 1)
    output = (residual_part.astype(jnp.float32) + mine).astype(jnp.bfloat16)
    return (output, cache)


def solution(mesh):
    placed = (
        P("tok", None),
        P(),
        P("tok", None),
        P(),
        P(),
        P(None, "tok", "mdl"),
        P(None, "tok", "mdl"),
        P(None, "mdl", "tok"),
        P("tok"),
    )
    return jax.shard_map(
        local,
        mesh=mesh,
        in_specs=placed,
        out_specs=(P("tok", "mdl"), P("tok", None, None, "mdl")),
        check_vma=False,
    )
```

profile of v0, /device:TPU:4, one launch (start us, length us, event | category | flops | bytes accessed | tf_op | source)
XLA Modules:
  0.0 475.9 jit_solution(12940662665245141497)
XLA Ops:
  11.6 35.2 %all-gather.5.cloned.1.call-done = bf16[2,2048,128]{2,1,0:T(8,128)(2,1)} async-done(((bf16[2,128,128]{2,1,0:T(8,128)(2,1)}), bf16[2,2048,128]{2,1,0:T(8,128)(2,1)}) %all-gather.5.cloned.1.call-update) | async-done | bytes 1048592 | tf_op jit(solution)/shard_map/all_gather | solution.py:87
  46.8 2.6 fusion.45
  50.9 6.2 %gather_fusion = s32[1024]{0:T(1024)S(1)} fusion(s32[8192]{0:T(1024)S(1)} %copy-done.2, s32[1024]{0:T(1024)S(1)} %broadcast_clamp_fusion.2), kind=kCustom, calls=%fused_computation | custom fusion | bytes 12288 | tf_op jit(solution)/shard_map/gather | solution.py:97
  57.4 2.3 reduce-window.6
  60.2 7.6 %scatter_custom_fusion.1 = bf16[2048]{0:T(1024)(128)(2,1)S(1)} fusion(s32[1024]{0:T(1024)S(1)} %bitcast.131, bf16[1024]{0:T(1024)(128)(2,1)S(1)} %broadcast.244, bf16[]{:T(256)} %constant.112.clone.1), kind=kCustom, calls=%fused_computation.125 | custom fusion | bytes 4098 | tf_op jit(solution)/shard_map/scatter | solution.py:83
  67.9 4.3 scatter_custom_fusion
  74.4 11.0 %gather_fusion.1 = bf16[2048,2048]{1,0:T(8,128)(2,1)} fusion(bf16[512,2048]{1,0:T(8,128)(2,1)S(1)} %fusion.36, s32[2048]{0:T(1024)S(1)} %get-tuple-element.163), kind=kCustom, calls=%fused_computation.1 | custom fusion | bytes 16785408 | tf_op jit(solution)/shard_map/gather | solution.py:85
  85.5 4.5 scatter_custom_fusion.2
  90.0 7.0 %fusion.42 = bf16[8,256,128]{2,1,0:T(8,128)(2,1)S(1)} fusion(bf16[8,2048,128]{2,1,0:T(8,128)(2,1)} %all-gather.9.cloned.1.call-done, bf16[8,256,2048]{2,1,0:T(8,128)(2,1)} %bitcast.113, bf16[8,256]{1,0:T(8,128)(2,1)S(1)} %mul.112), kind=kOutput, calls=%fused_computation.68 | convolution fusion | flops 1078198272 | bytes 13111296 | tf_op jit(solution)/shard_map/ecd,edh->ech/dot_general | solution.py:88
  97.0 3.2 gather_fusion.2
  100.2 30.9 %all-gather.7.cloned.1.call-done = bf16[8192,2,128]{2,0,1:T(8,128)(2,1)} async-done(((bf16[512,2,128]{2,0,1:T(8,128)(2,1)}), bf16[8192,2,128]{2,0,1:T(8,128)(2,1)}) %all-gather.7.cloned.1.call-update) | async-done | bytes 4194320 | tf_op jit(solution)/shard_map/all_gather | solution.py:109
  131.1 3.8 fusion.71
  134.9 73.6 %while.15 = (s32[]{:T(128)}, f32[1,1024]{1,0:T(1,128)S(1)}, f32[1,1024]{1,0:T(1,128)S(1)}, f32[1,1024,128]{2,1,0:T(8,128)S(1)}, s32[16]{0:T(128)S(1)}, /*index=5...) while((s32[]{:T(128)}, f32[1,1024]{1,0:T(1,128)S(1)}, ...), condition=%wide.region_11.12_spmd.clone, body=%wide.region_8.11_spmd.clone.sunk | while | flops 280377856 | bytes 7966885 | solution.py:137
  208.8 6.2 %gather_fusion.3 = bf16[2048,128]{1,0:T(8,128)(2,1)S(1)} fusion(bf16[1024,128]{1,0:T(8,128)(2,1)S(1)} %fusion.51, s32[2048]{0:T(1024)S(1)} %get-tuple-element.169), kind=kCustom, calls=%fused_computation.3 | custom fusion | bytes 1056768 | tf_op jit(solution)/shard_map/gather | solution.py:144
  215.0 4.6 fusion.48
  219.6 7.1 %bitcast_multiply_fusion = f32[2048,2048]{1,0:T(8,128)} fusion(f32[8,256,2048]{2,1,0:T(8,128)S(1)} %fusion.48, f32[2048]{0:T(1024)S(1)} %scatter_custom_fusion.2), kind=kLoop, calls=%fused_computation.55 | loop fusion | flops 4194304 | bytes 33562624 | tf_op jit(solution)/shard_map/mul | solution.py:153
  226.7 29.5 %scatter_custom_fusion.3 = f32[512,2048]{1,0:T(8,128)} fusion(s32[2048]{0:T(1024)S(1)} %get-tuple-element.164, f32[2048,2048]{1,0:T(8,128)} %bitcast_multiply_fusion, f32[]{:T(128)} %constant.102.clone.1), kind=kCustom, calls=%fused_computation.66 | custom fusion | flops 4194304 | bytes 4194816 | tf_op jit(solution)/shard_map/scatter-add | solution.py:153
  256.1 2.5 convert_element_type.51
  258.7 2.5 copy.41
  264.3 5.5 %all-to-all-start = ((s32[16,1,2]{2,1,0:T(1,128)}), s32[16,1,2]{2,1,0:T(1,128)S(1)}, u32[]{:S(2)}, u32[]{:S(2)}) async-start(s32[16,1,2]{2,1,0:T(1,128)} %bitcast.16), calls=%async_computation | async-start | bytes 16384 | tf_op jit(solution)/shard_map/all_to_all | solution.py:46
  271.1 2.4 all-to-all-done
  273.5 5.7 %all-to-all-start.1 = ((bf16[16,2,16,2,128]{4,2,3,1,0:T(8,128)(2,1)}), bf16[16,2,16,2,128]{4,2,3,1,0:T(8,128)(2,1)S(1)}, u32[]{:S(2)}, u32[]{:S(2)}) async-start(bf16[16,2,16,2,128]{4,2,3,1,0:T(8,128)(2,1)} %bitcast.19), calls=%async_computation.1 | async-start | bytes 524288 | tf_op jit(solution)/shard_map/all_to_all | solution.py:45
  279.4 4.8 %all-to-all-done.1 = bf16[16,2,16,2,128]{4,2,3,1,0:T(8,128)(2,1)S(1)} async-done(((bf16[16,2,16,2,128]{4,2,3,1,0:T(8,128)(2,1)}), bf16[16,2,16,2,128]{4,2,3,1,0:T(8,128)(2,1)S(1)}, u32[]{:S(2)}, u32[]{:S(2)}) %all-to-all-start.1) | async-done | bytes 262176 | tf_op jit(solution)/shard_map/all_to_all | solution.py:45
  286.7 180.0 %reduce-scatter.4.cloned.1.call-done = bf16[128,512]{1,0:T(8,128)(2,1)} async-done(((bf16[2048,512]{1,0:T(8,128)(2,1)}), bf16[128,512]{1,0:T(8,128)(2,1)}) %reduce-scatter.4.cloned.1.call-update) | async-done | bytes 131088
  (228 shorter events, 91.2 us)
Async XLA Ops:
  7.2 65.0 %copy-start = (f32[2048,8]{0,1:T(8,128)S(1)}, f32[2048,8]{0,1:T(8,128)}, u32[]{:S(2)}) copy-start(f32[2048,8]{0,1:T(8,128)} %param.15) | copy-start | bytes 196612
  7.2 3.8 copy-start.7
  7.2 39.6 %all-gather.5.cloned.1.call-start = ((), (), s32[]{:S(2)}) async-start(), calls=%async_computation.3 | async-start | bytes 1114112 | tf_op jit(solution)/shard_map/all_gather | solution.py:87
  7.9 82.1 %all-gather.9.cloned.1.call-start = ((), (), s32[]{:S(2)}) async-start(), calls=%async_computation.5 | async-start | bytes 4456448 | tf_op jit(solution)/shard_map/all_gather | solution.py:86
  8.7 122.4 %all-gather.7.cloned.1.call-start = ((), (), s32[]{:S(2)}) async-start(), calls=%async_computation.4 | async-start | bytes 4456448 | tf_op jit(solution)/shard_map/all_gather | solution.py:109
  8.7 2.3 copy-start.4
  11.5 38.6 %copy-start.6 = (s32[512,2]{0,1:T(2,128)S(1)}, s32[512,2]{0,1:T(2,128)}, u32[]{:S(2)}) copy-start(s32[512,2]{0,1:T(2,128)} %param.13) | copy-start | bytes 12292
  11.5 39.1 %copy-start.2 = (s32[8192]{0:T(1024)S(1)}, s32[8192]{0:T(1024)}, u32[]{:S(2)}) copy-start(s32[8192]{0:T(1024)} %param.12) | copy-start | bytes 98308
  49.4 165.5 %all-gather.11.cloned.1.call-start = ((), (), s32[]{:S(2)}) async-start(), calls=%async_computation.6 | async-start | bytes 4456448 | tf_op jit(solution)/shard_map/all_gather | solution.py:147
  50.0 416.7 %reduce-scatter.4.cloned.1.call-start = ((), (), s32[]{:S(2)}) async-start(), calls=%async_computation.7 | async-start | bytes 2228224
  261.2 0.7 copy-start.3
  261.2 8.7 %copy-start.5 = (bf16[512,2,128]{2,0,1:T(8,128)(2,1)S(1)}, bf16[512,2,128]{2,0,1:T(8,128)(2,1)}, u32[]{:S(2)}) copy-start(bf16[512,2,128]{2,0,1:T(8,128)(2,1)} %fusion.45) | copy-start | bytes 786436
  261.8 207.6 %copy-start.1 = (f32[2048,8]{0,1:T(8,128)S(1)}, f32[2048,8]{0,1:T(8,128)}, u32[]{:S(2)}) copy-start(f32[2048,8]{0,1:T(8,128)} %param.15) | copy-start | bytes 196612
  264.3 9.3 %all-to-all-start = ((s32[16,1,2]{2,1,0:T(1,128)}), s32[16,1,2]{2,1,0:T(1,128)S(1)}, u32[]{:S(2)}, u32[]{:S(2)}) async-start(s32[16,1,2]{2,1,0:T(1,128)} %bitcast.16), calls=%async_computation | async-start | bytes 16384 | tf_op jit(solution)/shard_map/all_to_all | solution.py:46
  273.5 10.7 %all-to-all-start.1 = ((bf16[16,2,16,2,128]{4,2,3,1,0:T(8,128)(2,1)}), bf16[16,2,16,2,128]{4,2,3,1,0:T(8,128)(2,1)S(1)}, u32[]{:S(2)}, u32[]{:S(2)}) async-start(bf16[16,2,16,2,128]{4,2,3,1,0:T(8,128)(2,1)} %bitcast.19), calls=%async_computation.1 | async-start | bytes 524288 | tf_op jit(solution)/shard_map/all_to_all | solution.py:45
Sparse Core Ops, SparseCore 0:
  9.8 36.9 all-gather.4
  48.6 40.0 all-gather.8
  91.0 40.0 all-gather.6
  132.7 49.4 all-gather.10
  261.3 205.3 reduce-scatter.3
where the time goes:
time: 477 us; the launch traced here: 476 us
  waiting for transfers between devices  255 us (53%)
  other arithmetic  69.7 us (15%)
  local copies, waits for them, and re-layouts  67.9 us (14%)
  matrix products  56.2 us (12%)
  between operations  14.2 us (3%)
  starting transfers between devices  11.4 us (2%)
    unnamed x6, waiting for transfers between devices  182 us
    all_gather x1, waiting for transfers between devices, local(): key_part = lax.all_gather(kv_weight, 'tok', axis=1, tiled=True)  35.2 us
    all_gather x1, waiting for transfers between devices, local(): piece = lax.all_gather(key_values, 'tok', axis=0, tiled=True)  30.9 us
    scatter-add x1, other arithmetic, local(): jnp.zeros((tok_dev, count), jnp.float32).at[slot_token]  29.5 us
    dot_general x16, matrix products, one_block(): jnp.einsum('hqd,khd->hqk', by_head_q, key_block, preferred_element_type=j...  24.3 us
    dot_general x16, matrix products, one_block(): jnp.einsum('hqk,khd->hqd', expon.astype(jnp.bfloat16), value_block, prefe...  16 us
    reduce_sum x16, other arithmetic, one_block(): total = total * shrink + jnp.sum(expon, axis=-1)  12.1 us
    gather x1, local copies, waits for them, and re-layouts, local(): normed[slot_token] * slot_filled[:, None]  11 us
  transfers between devices with their start and end apart: 7, of which 5 were waited for; matrix products, arithmetic and copies ran while one was open for 30% of the time, Pallas kernels for 0%

commit v1 on v0

--- a/solution.py
+++ b/solution.py
@@ -83,8 +83,13 @@
     slot_filled = jnp.zeros((experts * capacity,), jnp.bfloat16).at[slots].set(jnp.bfloat16(1.0))
     slot_gate = jnp.zeros((experts * capacity,), jnp.float32).at[slots].set(gates.reshape(-1))
     grouped = (normed[slot_token] * slot_filled[:, None]).reshape(experts, capacity, width)
-    query_part = lax.all_gather(query_weight, "tok", axis=1, tiled=True)
-    key_part = lax.all_gather(kv_weight, "tok", axis=1, tiled=True)
+    query_part, key_part = jnp.split(
+        lax.all_gather(
+            jnp.concatenate([query_weight, kv_weight], axis=0), "tok", axis=1, tiled=True
+        ),
+        [query_weight.shape[0]],
+        axis=0,
+    )
     query_total = jnp.einsum(
         "ecd,edh->ech", grouped, query_part, preferred_element_type=jnp.float32
     )

time: 477 us -> 452 us (0.948)
  waiting for transfers between devices: 255 us -> 230 us
    all_gather x1, waiting for transfers between devices: 30.9 us -> 0.02 us  [local(): piece = lax.all_gather(key_values, 'tok', axis=0, tiled=True)]
    all_gather x2 -> x1, waiting for transfers between devices: 35.2 us -> 41.6 us  [local(): lax.all_gather(jnp.concatenate([query_weight, kv_weight], axis=0), 'tok',...]
    unnamed x6 -> x5, waiting for transfers between devices: 182 us -> 181 us
  transfers between devices with their start and end apart: 7 -> 6, of which waited for: 5 -> 4; matrix products, arithmetic and copies ran while one was open for 30% -> 31% of each run, Pallas kernels for 0% -> 0%
where the time goes in v1:
time: 452 us; the launch traced here: 451 us
  waiting for transfers between devices  230 us (51%)
  other arithmetic  70.5 us (16%)
  local copies, waits for them, and re-layouts  67.8 us (15%)
  matrix products  56.2 us (12%)
  between operations  14.2 us (3%)
  starting transfers between devices  10.9 us (2%)
    unnamed x5, waiting for transfers between devices  181 us
    all_gather x1, waiting for transfers between devices, local(): lax.all_gather(jnp.concatenate([query_weight, kv_weight], axis=0), 'tok',...  41.6 us
    scatter-add x1, other arithmetic, local(): jnp.zeros((tok_dev, count), jnp.float32).at[slot_token]  29.5 us
    dot_general x16, matrix products, one_block(): jnp.einsum('hqd,khd->hqk', by_head_q, key_block, preferred_element_type=j...  24.3 us
    dot_general x16, matrix products, one_block(): jnp.einsum('hqk,khd->hqd', expon.astype(jnp.bfloat16), value_block, prefe...  16 us
    reduce_sum x16, other arithmetic, one_block(): total = total * shrink + jnp.sum(expon, axis=-1)  12.1 us
    gather x1, local copies, waits for them, and re-layouts, local(): normed[slot_token] * slot_filled[:, None]  11 us
    dynamic_slice x16, local copies, waits for them, and re-layouts, local(): state, _ = lax.scan(one_block, state, (key_blocks, value_blocks, firsts))  9.42 us
  transfers between devices with their start and end apart: 6, of which 4 were waited for; matrix products, arithmetic and copies ran while one was open for 31% of the time, Pallas kernels for 0%

profile of v1, /device:TPU:4, one launch (start us, length us, event | category | flops | bytes accessed | tf_op | source)
XLA Modules:
  0.0 450.9 jit_solution(4743075321639211674)
XLA Ops:
  9.1 2.2 fusion.34
  11.9 41.6 %all-gather.4.cloned.1.call-done = bf16[10,2048,128]{2,1,0:T(8,128)(2,1)} async-done(((bf16[10,128,128]{2,1,0:T(8,128)(2,1)}), bf16[10,2048,128]{2,1,0:T(8,128)(2,1)}) %all-gather.4.cloned.1.call-update) | async-done | bytes 5242896 | tf_op jit(solution)/shard_map/all_gather | solution.py:87
  53.5 2.6 fusion.48
  57.7 6.2 %gather_fusion = s32[1024]{0:T(1024)S(1)} fusion(s32[8192]{0:T(1024)S(1)} %copy-done.2, s32[1024]{0:T(1024)S(1)} %broadcast_clamp_fusion.2), kind=kCustom, calls=%fused_computation | custom fusion | bytes 12288 | tf_op jit(solution)/shard_map/gather | solution.py:102
  64.2 2.3 reduce-window.6
  67.1 7.6 %scatter_custom_fusion.1 = bf16[2048]{0:T(1024)(128)(2,1)S(1)} fusion(s32[1024]{0:T(1024)S(1)} %bitcast.129, bf16[1024]{0:T(1024)(128)(2,1)S(1)} %broadcast.244, bf16[]{:T(256)} %constant.112.clone.1), kind=kCustom, calls=%fused_computation.128 | custom fusion | bytes 4098 | tf_op jit(solution)/shard_map/scatter | solution.py:83
  74.7 4.3 scatter_custom_fusion
  81.3 11.0 %gather_fusion.1 = bf16[2048,2048]{1,0:T(8,128)(2,1)} fusion(bf16[512,2048]{1,0:T(8,128)(2,1)S(1)} %fusion.36, s32[2048]{0:T(1024)S(1)} %get-tuple-element.163), kind=kCustom, calls=%fused_computation.1 | custom fusion | bytes 16785408 | tf_op jit(solution)/shard_map/gather | solution.py:85
  92.3 4.5 scatter_custom_fusion.2
  96.8 7.0 %fusion.43 = bf16[8,256,128]{2,1,0:T(8,128)(2,1)S(1)} fusion(bf16[10,2048,128]{2,1,0:T(8,128)(2,1)} %all-gather.4.cloned.1.call-done, bf16[8,256,2048]{2,1,0:T(8,128)(2,1)} %bitcast.111, bf16[8,256]{1,0:T(8,128)(2,1)S(1)} %mul.112), kind=kOutput, calls=%fused_computation.69 | convolution fusion | flops 1078198272 | bytes 13111296 | tf_op jit(solution)/shard_map/ecd,edh->ech/dot_general | solution.py:93
  103.8 3.2 gather_fusion.2
  107.1 3.8 fusion.75
  110.9 72.7 %while.15 = (s32[]{:T(128)}, f32[1,1024]{1,0:T(1,128)S(1)}, f32[1,1024]{1,0:T(1,128)S(1)}, f32[1,1024,128]{2,1,0:T(8,128)S(1)}, s32[16]{0:T(128)S(1)}, /*index=5...) while((s32[]{:T(128)}, f32[1,1024]{1,0:T(1,128)S(1)}, ...), condition=%wide.region_11.12_spmd.clone, body=%wide.region_8.11_spmd.clone.sunk | while | flops 280377856 | bytes 7966885 | solution.py:142
  183.8 6.2 %gather_fusion.3 = bf16[2048,128]{1,0:T(8,128)(2,1)S(1)} fusion(bf16[1024,128]{1,0:T(8,128)(2,1)S(1)} %fusion.55, s32[2048]{0:T(1024)S(1)} %get-tuple-element.169), kind=kCustom, calls=%fused_computation.3 | custom fusion | bytes 1056768 | tf_op jit(solution)/shard_map/gather | solution.py:149
  190.0 4.6 %fusion.52 = f32[8,256,2048]{2,1,0:T(8,128)S(1)} fusion(bf16[8,128,2048]{2,1,0:T(8,128)(2,1)} %all-gather.8.cloned.1.call-done, bf16[8,256,128]{2,1,0:T(8,128)(2,1)S(1)} %bitcast.114, bf16[8,256]{1,0:T(8,128)(2,1)S(1)} %mul.112), kind=kOutput, calls=%fused_computation.72 | convolution fusion | flops 1074003968 | bytes 21499904 | tf_op jit(solution)/shard_map/ech,ehn->ecn/dot_general | solution.py:154
  194.6 7.1 %bitcast_multiply_fusion = f32[2048,2048]{1,0:T(8,128)} fusion(f32[8,256,2048]{2,1,0:T(8,128)S(1)} %fusion.52, f32[2048]{0:T(1024)S(1)} %scatter_custom_fusion.2), kind=kLoop, calls=%fused_computation.55 | loop fusion | flops 4194304 | bytes 33562624 | tf_op jit(solution)/shard_map/mul | solution.py:158
  201.7 29.5 %scatter_custom_fusion.3 = f32[512,2048]{1,0:T(8,128)} fusion(s32[2048]{0:T(1024)S(1)} %get-tuple-element.164, f32[2048,2048]{1,0:T(8,128)} %bitcast_multiply_fusion, f32[]{:T(128)} %constant.102.clone.1), kind=kCustom, calls=%fused_computation.67 | custom fusion | flops 4194304 | bytes 4194816 | tf_op jit(solution)/shard_map/scatter-add | solution.py:158
  231.2 2.5 convert_element_type.51
  233.7 2.5 copy.41
  239.3 5.1 %all-to-all-start = ((s32[16,1,2]{2,1,0:T(1,128)}), s32[16,1,2]{2,1,0:T(1,128)S(1)}, u32[]{:S(2)}, u32[]{:S(2)}) async-start(s32[16,1,2]{2,1,0:T(1,128)} %bitcast.16), calls=%async_computation | async-start | bytes 16384 | tf_op jit(solution)/shard_map/all_to_all | solution.py:46
  245.7 2.4 all-to-all-done
  248.1 5.7 %all-to-all-start.1 = ((bf16[16,2,16,2,128]{4,2,3,1,0:T(8,128)(2,1)}), bf16[16,2,16,2,128]{4,2,3,1,0:T(8,128)(2,1)S(1)}, u32[]{:S(2)}, u32[]{:S(2)}) async-start(bf16[16,2,16,2,128]{4,2,3,1,0:T(8,128)(2,1)} %bitcast.19), calls=%async_computation.1 | async-start | bytes 524288 | tf_op jit(solution)/shard_map/all_to_all | solution.py:45
  253.9 4.8 %all-to-all-done.1 = bf16[16,2,16,2,128]{4,2,3,1,0:T(8,128)(2,1)S(1)} async-done(((bf16[16,2,16,2,128]{4,2,3,1,0:T(8,128)(2,1)}), bf16[16,2,16,2,128]{4,2,3,1,0:T(8,128)(2,1)S(1)}, u32[]{:S(2)}, u32[]{:S(2)}) %all-to-all-start.1) | async-done | bytes 262176 | tf_op jit(solution)/shard_map/all_to_all | solution.py:45
  261.3 180.4 %reduce-scatter.4.cloned.1.call-done = bf16[128,512]{1,0:T(8,128)(2,1)} async-done(((bf16[2048,512]{1,0:T(8,128)(2,1)}), bf16[128,512]{1,0:T(8,128)(2,1)}) %reduce-scatter.4.cloned.1.call-update) | async-done | bytes 131088
  (226 shorter events, 88.5 us)
Async XLA Ops:
  7.2 71.9 %copy-start = (f32[2048,8]{0,1:T(8,128)S(1)}, f32[2048,8]{0,1:T(8,128)}, u32[]{:S(2)}) copy-start(f32[2048,8]{0,1:T(8,128)} %param.15) | copy-start | bytes 196612
  7.2 4.1 copy-start.7
  7.2 46.3 %all-gather.4.cloned.1.call-start = ((), (), s32[]{:S(2)}) async-start(), calls=%async_computation.3 | async-start | bytes 5570560 | tf_op jit(solution)/shard_map/all_gather | solution.py:87
  9.0 98.1 %all-gather.6.cloned.1.call-start = ((), (), s32[]{:S(2)}) async-start(), calls=%async_computation.4 | async-start | bytes 4456448 | tf_op jit(solution)/shard_map/all_gather | solution.py:114
  9.0 2.3 copy-start.4
  11.9 45.1 %copy-start.6 = (s32[512,2]{0,1:T(2,128)S(1)}, s32[512,2]{0,1:T(2,128)}, u32[]{:S(2)}) copy-start(s32[512,2]{0,1:T(2,128)} %param.13) | copy-start | bytes 12292
  11.9 45.6 %copy-start.2 = (s32[8192]{0:T(1024)S(1)}, s32[8192]{0:T(1024)}, u32[]{:S(2)}) copy-start(s32[8192]{0:T(1024)} %param.12) | copy-start | bytes 98308
  56.2 133.8 %all-gather.8.cloned.1.call-start = ((), (), s32[]{:S(2)}) async-start(), calls=%async_computation.5 | async-start | bytes 4456448 | tf_op jit(solution)/shard_map/all_gather | solution.py:152
  56.9 384.8 %reduce-scatter.4.cloned.1.call-start = ((), (), s32[]{:S(2)}) async-start(), calls=%async_computation.6 | async-start | bytes 2228224
  236.2 0.7 copy-start.3
  236.2 8.2 %copy-start.5 = (bf16[512,2,128]{2,0,1:T(8,128)(2,1)S(1)}, bf16[512,2,128]{2,0,1:T(8,128)(2,1)}, u32[]{:S(2)}) copy-start(bf16[512,2,128]{2,0,1:T(8,128)(2,1)} %fusion.48) | copy-start | bytes 786436
  236.9 207.5 %copy-start.1 = (f32[2048,8]{0,1:T(8,128)S(1)}, f32[2048,8]{0,1:T(8,128)}, u32[]{:S(2)}) copy-start(f32[2048,8]{0,1:T(8,128)} %param.15) | copy-start | bytes 196612
  239.3 8.8 %all-to-all-start = ((s32[16,1,2]{2,1,0:T(1,128)}), s32[16,1,2]{2,1,0:T(1,128)S(1)}, u32[]{:S(2)}, u32[]{:S(2)}) async-start(s32[16,1,2]{2,1,0:T(1,128)} %bitcast.16), calls=%async_computation | async-start | bytes 16384 | tf_op jit(solution)/shard_map/all_to_all | solution.py:46
  248.1 10.7 %all-to-all-start.1 = ((bf16[16,2,16,2,128]{4,2,3,1,0:T(8,128)(2,1)}), bf16[16,2,16,2,128]{4,2,3,1,0:T(8,128)(2,1)S(1)}, u32[]{:S(2)}, u32[]{:S(2)}) async-start(bf16[16,2,16,2,128]{4,2,3,1,0:T(8,128)(2,1)} %bitcast.19), calls=%async_computation.1 | async-start | bytes 524288 | tf_op jit(solution)/shard_map/all_to_all | solution.py:45
Sparse Core Ops, SparseCore 0:
  9.8 43.6 all-gather.3
  56.3 40.2 all-gather.5
  98.3 49.4 all-gather.7
  236.4 205.3 reduce-scatter.3
